TPU v7x, 32 devices: a whole 2x2x4 slice. The times are simulated.
32 devices in a mesh: groups: 2 (over x), frames: 16 (over z, y, core).
Axes of the slice: x: 2, y: 2, z: 4, core: 2. Of those that a mesh axis runs over, the one named last changes fastest.
Arguments:
- video: bfloat16 [4, 16, 128, 1024], P('groups', 'frames'), parts along dimension 0, may hold values from -70 to 70
- w_qkv: bfloat16 [1024, 3072], replicated, may hold values from -8 to 8
- w_out: bfloat16 [1024, 1024], replicated, may hold values from -0.1875 to 0.1875
- keep_list: int32 [4, 16, 128], P('groups', 'frames'), parts along dimension 0, may hold values from 0 to 127, each once within a row
- kept_counts: int32 [4, 16], P('groups', 'frames'), parts along dimension 0, may hold values from 1 to 4, 32 in all within a row
- w_proj: bfloat16 [1024, 8192], P(None, 'frames'), may hold values from -20 to 20
- llm_gain: bfloat16 [8192], P('frames'), may hold values from 0.099609375 to 1.8984375
- w_gate: bfloat16 [8192, 16384], P(None, 'frames'), may hold values from -0.0625 to 0.0625
- w_up: bfloat16 [8192, 16384], P(None, 'frames'), may hold values from -0.0625 to 0.0625
Outputs:
- llm_hidden: bfloat16 [4, 32, 16384], P('groups', None, 'frames'), parts along dimension 0
There are 2 independent parts, one for each index of `groups`. A program takes and returns all parts, laid end to end along the dimension named above; an argument that names none is the same for every part. Nothing has to cross between parts.
Inputs may be any that keep to these rules, and one draw needn't show every extreme that they name: `keep_list`: each row of a frame lists every patch index once. `kept_counts`: the counts of one video sum to 32.
All inputs are finite; a program needn't handle non-finite values. No bound on the sum of `kept_counts` on one device may be relied on, other than what follows from the above.
Results may differ from a plain program's by a relative error of at most 0.0076.
Values may be sent and summed in bfloat16 or wider, within the bound.
No kernel may reach another device: no remote copies, remote signals or barrier semaphores. Data moves between devices by JAX's collectives and lax.ppermute only.
A program may use at most 128 MiB of HBM per device.

v0:
```python
import jax
import jax.numpy as jnp
from jax import lax
from jax.sharding import PartitionSpec as P

HEAD_DIM = 64
DL = 8192
TOKL = 2
KMAX = 4
NORM_EPS = 1e-05
SCORE_SCALE = 0.125


def layer_norm(values):
    floated = values.astype(jnp.float32)
    average = jnp.mean(floated, axis=-1, keepdims=True)
    centred = floated - average
    variance = jnp.mean(centred * centred, axis=-1, keepdims=True)
    return (centred * lax.rsqrt(variance + NORM_EPS)).astype(jnp.bfloat16)


def sequence_slots(counts, seq_len, slot_width):
    offsets = jnp.cumsum(counts, axis=1) - counts
    positions = lax.broadcasted_iota(jnp.int32, (counts.shape[0], seq_len), 1)
    started = (offsets[:, None, :] <= positions[:, :, None]).astype(jnp.int32)
    owner_frame = jnp.sum(started, axis=2) - 1
    frame_ids = lax.broadcasted_iota(jnp.int32, started.shape, 2)
    begin_at = jnp.sum(
        jnp.where(frame_ids == owner_frame[:, :, None], offsets[:, None, :], 0), axis=2
    )
    return owner_frame * slot_width + positions - begin_at


def temporal_attention(queries, keys_in, values_in):
    scores = (
        jnp.einsum("vfphe,vgphe->vphfg", queries, keys_in, preferred_element_type=jnp.float32)
        * SCORE_SCALE
    )
    largest = jnp.max(scores, axis=-1, keepdims=True)
    weights_exp = jnp.exp(scores - largest)
    weights = (weights_exp / jnp.sum(weights_exp, axis=-1, keepdims=True)).astype(jnp.bfloat16)
    return jnp.einsum(
        "vphfg,vgphe->vfphe", weights, values_in, preferred_element_type=jnp.float32
    ).astype(jnp.bfloat16)


def take_frame_rows(frame_rows, picks_row):
    return jnp.take(frame_rows, picks_row, axis=0)


def local(video, w_qkv, w_out, keep_list, kept_counts, w_proj, llm_gain, w_gate, w_up):
    videos = video.shape[0]
    patches = video.shape[2]
    model_width = video.shape[3]
    devices = lax.axis_size("frames")
    head_count = model_width // HEAD_DIM
    all_counts = lax.all_gather(kept_counts, "frames", axis=1, tiled=True)
    normed = layer_norm(video)

    def split_heads(tensor_in):
        return tensor_in.reshape(tensor_in.shape[:3] + (head_count, HEAD_DIM))

    received = lax.all_to_all(normed, "frames", split_axis=2, concat_axis=1, tiled=True)
    projected_here = jnp.dot(
        received.reshape(-1, model_width), w_qkv, preferred_element_type=jnp.float32
    ).astype(jnp.bfloat16)
    projected_here = projected_here.reshape(received.shape[:3] + (3 * model_width,))
    queries = split_heads(projected_here[..., :model_width])
    keys_in = split_heads(projected_here[..., model_width : 2 * model_width])
    values_in = split_heads(projected_here[..., 2 * model_width :])
    attended = temporal_attention(queries, keys_in, values_in)
    attended = attended.reshape(projected_here.shape[:3] + (model_width,))
    returned = lax.all_to_all(attended, "frames", split_axis=1, concat_axis=2, tiled=True)
    encoded = (
        video.astype(jnp.float32).reshape(-1, model_width)
        + jnp.dot(returned.reshape(-1, model_width), w_out, preferred_element_type=jnp.float32)
    ).astype(jnp.bfloat16)
    encoded = encoded.reshape(videos, patches, model_width)
    chosen = keep_list[:, 0, :KMAX]
    picked = jax.vmap(take_frame_rows)(encoded, chosen)
    slot_index = lax.broadcasted_iota(jnp.int32, (videos, KMAX), 1)
    live_slots = slot_index < kept_counts
    slot_rows = jnp.where(live_slots[:, :, None], picked, jnp.zeros_like(picked))
    gathered_slots = lax.all_gather(slot_rows, "frames", axis=1, tiled=True)
    sequence_order = sequence_slots(all_counts, devices * TOKL, KMAX)
    local_cols = jnp.dot(
        gathered_slots.reshape(-1, model_width), w_proj, preferred_element_type=jnp.float32
    )
    local_cols = local_cols.reshape(gathered_slots.shape[0], gathered_slots.shape[1], -1)
    squares = lax.psum(jnp.sum(local_cols * local_cols, axis=2), "frames")
    row_scale = lax.rsqrt(squares / DL + NORM_EPS)
    normed_cols = (local_cols * row_scale[:, :, None] * llm_gain.astype(jnp.float32)).astype(
        jnp.bfloat16
    )
    hidden_width = w_gate.shape[1]
    zero_sums = jnp.zeros(
        (gathered_slots.shape[0], gathered_slots.shape[1], hidden_width), jnp.float32
    )
    column_piece = lax.all_gather(normed_cols, "frames", axis=2, tiled=True)
    piece_width = column_piece.shape[2]
    flat_piece = column_piece.reshape(-1, piece_width)
    gate_more = jnp.dot(flat_piece, w_gate, preferred_element_type=jnp.float32).reshape(
        zero_sums.shape
    )
    up_more = jnp.dot(flat_piece, w_up, preferred_element_type=jnp.float32).reshape(zero_sums.shape)
    hidden_slots = (jax.nn.silu(gate_more) * up_more).astype(jnp.bfloat16)
    llm_hidden = jax.vmap(take_frame_rows)(hidden_slots, sequence_order)
    return llm_hidden


def solution(mesh):
    in_specs = (
        P("groups", "frames", None, None),
        P(),
        P(),
        P("groups", "frames", None),
        P("groups", "frames"),
        P(None, "frames"),
        P("frames"),
        P(None, "frames"),
        P(None, "frames"),
    )
    out_specs = P("groups", None, "frames")
    return jax.shard_map(local, mesh=mesh, in_specs=in_specs, out_specs=out_specs, check_vma=False)
```

profile of v0, /device:TPU:0, one launch (start us, length us, event | category | flops | bytes accessed | tf_op | source)
XLA Modules:
  0.0 195.9 jit_solution(10785479989955932589)
XLA Ops:
  6.5 0.0 copy-start
  6.5 1.7 convert_reduce_fusion
  8.3 1.9 multiply_reduce_fusion.1
  10.2 1.7 multiply_convert_fusion
  12.0 21.5 %all_to_all.8 = bf16[2,1,128,1024]{3,0,1,2:T(2,128)(2,1)S(1)} all-to-all(bf16[2,1,128,1024]{3,0,1,2:T(2,128)(2,1)S(1)} %multiply_convert_fusion), channel_id=1, replica_groups=mesh['groups'=2,'frames'=16] {'frames'}, dimensions={2} | all-to-all | bytes 1048576 | tf_op jit(solution)/shard_map/all_to_all | solution.py:63
  33.5 0.1 copy.62
  33.6 4.6 %convolution_convert_fusion = bf16[256,3072]{1,0:T(8,128)(2,1)S(1)} fusion(bf16[256,1024]{1,0:T(8,128)(2,1)S(1)} %bitcast.65, bf16[1024,3072]{1,0:T(8,128)(2,1)} %param.10), kind=kOutput, calls=%fused_computation.7 | convolution fusion | flops 1611399168 | bytes 8388608 | tf_op jit(solution)/shard_map/dot_general | solution.py:64
  38.2 0.9 fusion.42
  39.1 2.5 %reshape.177 = bf16[2,16,8,16,64]{4,3,2,1,0:T(8,128)(2,1)} reshape(bf16[2,16,8,1024]{3,2,1,0:T(8,128)(2,1)} %get-tuple-element.7) | data formatting | bytes 1048576 | tf_op jit(solution)/shard_map/reshape | solution.py:61
  41.6 1.6 reshape.178
  43.2 1.6 reshape.176
  44.9 0.0 copy-start.3
  44.9 4.9 %fusion.43 = (f32[2,8,16,16]{3,2,1,0:T(8,128)S(1)}, f32[2,8,16,16,16]{3,4,2,1,0:T(8,128)}) fusion(bf16[2,16,8,16,64]{4,3,2,1,0:T(8,128)(2,1)} %reshape.178, bf16[2,16,8,16,64]{4,3,2,1,0:T(8,128)(2,1)} %reshape.177), kind=kOutput, calls=%fused_computation.62 | convolution fusion | flops 8585231 | bytes 1327104 | tf_op jit(solution)/shard_map/sub | solution.py:40
  49.8 0.0 copy-done.3
  49.8 2.5 %fusion.6 = bf16[2,16,8,16,64]{4,1,3,2,0:T(8,128)(2,1)S(1)} fusion(f32[2,8,16,16,16]{3,4,2,1,0:T(8,128)} %get-tuple-element.9, bf16[2,16,8,16,64]{4,3,2,1,0:T(8,128)(2,1)S(1)} %copy-done.3, f32[2,8,16,16]{3,2,1,0:T(8,128)S(1)} %get-tuple-element.8), kind=kOutput, calls=%fused_computation.13 | convolution fusion | flops 8781824 | bytes 1327104 | tf_op jit(solution)/shard_map/vphfg,vgphe->vfphe/dot_general | solution.py:42
  52.2 0.0 copy-start.2
  52.3 1.3 copy.73
  53.5 2.6 %reshape.201 = bf16[2,16,8,1024]{3,2,0,1:T(8,128)(2,1)} reshape(bf16[2,16,8,16,64]{4,3,2,0,1:T(8,128)(2,1)} %copy.73) | data formatting | bytes 1048576 | tf_op jit(solution)/shard_map/reshape | solution.py:72
  56.1 4.2 %all-to-all-start.1 = ((bf16[2,16,8,1024]{3,2,0,1:T(8,128)(2,1)}), bf16[2,16,8,1024]{3,2,0,1:T(8,128)(2,1)}, u32[]{:S(2)}, u32[]{:S(2)}) async-start(bf16[2,16,8,1024]{3,2,0,1:T(8,128)(2,1)} %reshape.201), calls=%async_computation.1 | async-start | bytes 1048576 | tf_op jit(solution)/shard_map/all_to_all | solution.py:73
  60.4 0.0 copy-start.5
  60.4 0.0 copy-start.4
  60.4 0.0 copy-start.6
  60.4 0.2 all-gather.3.cloned.1.call-start
  60.6 0.0 copy-done.2
  60.6 0.5 copy_convert_fusion
  61.2 0.3 copy.61
  61.5 0.0 copy-done.5
  61.6 0.1 reshape.182
  61.7 0.1 copy.59
  61.8 0.0 copy-done.4
  61.8 0.0 copy-done.6
  61.8 12.9 %all-to-all-done.1 = bf16[2,16,8,1024]{3,2,0,1:T(8,128)(2,1)} async-done(((bf16[2,16,8,1024]{3,2,0,1:T(8,128)(2,1)}), bf16[2,16,8,1024]{3,2,0,1:T(8,128)(2,1)}, u32[]{:S(2)}, u32[]{:S(2)}) %all-to-all-start.1) | async-done | bytes 524320 | tf_op jit(solution)/shard_map/all_to_all | solution.py:73
  74.7 1.1 copy.69
  75.7 0.0 copy-done
  75.8 1.5 fusion.7
  77.3 1.3 gather_fusion
  78.6 0.1 broadcast_select_fusion.2
  78.7 20.6 %all_gather.10 = bf16[2,64,1024]{2,0,1:T(2,128)(2,1)S(1)} all-gather(bf16[2,4,1024]{2,0,1:T(2,128)(2,1)S(1)} %broadcast_select_fusion.2), channel_id=1, replica_groups=mesh['groups'=2,'frames'=16] {'frames'}, dimensions={1}, use_global_device_ids=true | all-gather | bytes 278528 | tf_op jit(solution)/shard_map/all_gather | solution.py:84
  99.3 1.6 multiply_reduce_fusion.2
  100.9 29.8 %psum.7 = f32[2,64]{1,0:T(2,128)S(1)} all-reduce(f32[2,64]{1,0:T(2,128)S(1)} %get-tuple-element.10), channel_id=1, replica_groups=mesh['groups'=2,'frames'=16] {'frames'}, use_global_device_ids=true, to_apply=%region_8.9 | all-reduce | flops 128 | bytes 1024 | tf_op jit(solution)/shard_map/psum | solution.py:90
  130.7 0.8 multiply_convert_fusion.1
  131.5 0.0 all-gather.3.cloned.1.call-update
  131.5 17.1 %all-gather = s32[16,1,2]{2,1,0:T(1,128)S(1)} all-gather(s32[1,1,2]{2,1,0:T(1,128)S(1)} %bitcast.70), channel_id=1, replica_groups=mesh['groups'=2,'frames'=16] {'frames'}, dimensions={0}, use_global_device_ids=true | all-gather | bytes 136 | tf_op jit(solution)/shard_map/all_gather | solution.py:57
  148.7 0.1 copy.58
  148.7 0.2 reduce_window_sum.11
  148.9 0.1 convert_reduce_fusion.1
  149.0 0.1 select_reduce_fusion
  149.1 0.1 reshape.188
  149.2 20.7 %all-gather.3.cloned.1.call-done = bf16[2,64,8192]{2,1,0:T(8,128)(2,1)} async-done(((bf16[2,64,512]{2,1,0:T(8,128)(2,1)}), bf16[2,64,8192]{2,1,0:T(8,128)(2,1)}) %all-gather.3.cloned.1.call-update) | async-done | bytes 2097168 | tf_op jit(solution)/shard_map/all_gather | solution.py:99
  169.9 0.0 copy-start.1
  169.9 8.9 %fusion.3 = f32[2,64,1024]{2,1,0:T(8,128)S(1)} fusion(bf16[2,64,8192]{2,1,0:T(8,128)(2,1)} %all-gather.3.cloned.1.call-done, bf16[8192,1024]{1,0:T(8,128)(2,1)} %param.16), kind=kOutput, calls=%fused_computation.5 | convolution fusion | flops 2147483648 | bytes 19398656 | tf_op jit(solution)/shard_map/dot_general | solution.py:102
  178.8 0.0 copy-done.1
  178.8 8.3 %fusion.11 = bf16[2,64,1024]{2,1,0:T(8,128)(2,1)S(1)} fusion(bf16[2,64,8192]{2,1,0:T(8,128)(2,1)S(1)} %copy-done.1, bf16[8192,1024]{1,0:T(8,128)(2,1)} %param.17, f32[2,64,1024]{2,1,0:T(8,128)S(1)} %fusion.3), kind=kOutput, calls=%fused_computation.17 | convolution fusion | flops 2148270080 | bytes 19660800 | tf_op jit(solution)/shard_map/dot_general | solution.py:105
  187.2 1.1 gather_fusion.1
  188.3 0.7 broadcast_select_fusion
  (12 shorter events, 0.1 us)
Async XLA Ops:
  6.5 69.2 %copy-start = (bf16[1024,1024]{1,0:T(8,128)(2,1)S(1)}, bf16[1024,1024]{1,0:T(8,128)(2,1)}, u32[]{:S(2)}) copy-start(bf16[1024,1024]{1,0:T(8,128)(2,1)} %param.11) | copy-start | bytes 6291460
  44.9 4.9 %copy-start.3 = (bf16[2,16,8,16,64]{4,3,2,1,0:T(8,128)(2,1)S(1)}, bf16[2,16,8,16,64]{4,3,2,1,0:T(8,128)(2,1)}, u32[]{:S(2)}) copy-start(bf16[2,16,8,16,64]{4,3,2,1,0:T(8,128)(2,1)} %reshape.176) | copy-start | bytes 1572868
  52.2 8.4 %copy-start.2 = (bf16[2,1,128,1024]{3,2,1,0:T(8,128)(2,1)S(1)}, bf16[2,1,128,1024]{3,2,1,0:T(8,128)(2,1)}, u32[]{:S(2)}) copy-start(bf16[2,1,128,1024]{3,2,1,0:T(8,128)(2,1)} %param.9) | copy-start | bytes 1572868
  56.1 18.5 %all-to-all-start.1 = ((bf16[2,16,8,1024]{3,2,0,1:T(8,128)(2,1)}), bf16[2,16,8,1024]{3,2,0,1:T(8,128)(2,1)}, u32[]{:S(2)}, u32[]{:S(2)}) async-start(bf16[2,16,8,1024]{3,2,0,1:T(8,128)(2,1)} %reshape.201), calls=%async_computation.1 | async-start | bytes 1048576 | tf_op jit(solution)/shard_map/all_to_all | solution.py:73
  60.4 1.2 copy-start.5
  60.4 1.4 copy-start.4
  60.4 1.4 copy-start.6
  60.4 109.5 %all-gather.3.cloned.1.call-start = ((), (), s32[]{:S(2)}) async-start(), calls=%async_computation.2 | async-start | bytes 2228224 | tf_op jit(solution)/shard_map/all_gather | solution.py:99
  169.9 8.9 %copy-start.1 = (bf16[2,64,8192]{2,1,0:T(8,128)(2,1)S(1)}, bf16[2,64,8192]{2,1,0:T(8,128)(2,1)}, u32[]{:S(2)}) copy-start(bf16[2,64,8192]{2,1,0:T(8,128)(2,1)} %all-gather.3.cloned.1.call-done) | copy-start | bytes 6291460
Sparse Core Ops, SparseCore 0:
  131.6 38.2 all-gather.2
where the time goes:
time: 197 us; the launch traced here: 196 us
  blocking collectives  89.1 us (45%)
  waiting for transfers between devices  33.6 us (17%)
  matrix products  32.3 us (16%)
  local copies, waits for them, and re-layouts  14.9 us (8%)
  between operations  13.6 us (7%)
  other arithmetic  7.99 us (4%)
  starting transfers between devices  4.46 us (2%)
    psum x1, blocking collectives, local(): squares = lax.psum(jnp.sum(local_cols * local_cols, axis=2), 'frames')  29.8 us
    all_to_all x1, blocking collectives, local(): lax.all_to_all(normed, 'frames', split_axis=2, concat_axis=1, tiled=True)  21.5 us
    all_gather x1, waiting for transfers between devices, local(): column_piece = lax.all_gather(normed_cols, 'frames', axis=2, tiled=True)  20.7 us
    all_gather x1, blocking collectives, local(): gathered_slots = lax.all_gather(slot_rows, 'frames', axis=1, tiled=True)  20.6 us
    all_gather x1, blocking collectives, local(): all_counts = lax.all_gather(kept_counts, 'frames', axis=1, tiled=True)  17.1 us
    all_to_all x1, waiting for transfers between devices, local(): lax.all_to_all(attended, 'frames', split_axis=1, concat_axis=2, tiled=True)  12.9 us
    dot_general x1, matrix products, local(): jnp.dot(flat_piece, w_gate, preferred_element_type=jnp.float32)  8.87 us
    dot_general x1, matrix products, local(): jnp.dot(flat_piece, w_up, preferred_element_type=jnp.float32)  8.34 us
  transfers between devices with their start and end apart: 2, of which 2 were waited for; matrix products, arithmetic and copies ran while one was open for 1% of the time, Pallas kernels for 0%

commit v1 on v0

--- a/solution.py
+++ b/solution.py
@@ -81,7 +81,15 @@
     slot_index = lax.broadcasted_iota(jnp.int32, (videos, KMAX), 1)
     live_slots = slot_index < kept_counts
     slot_rows = jnp.where(live_slots[:, :, None], picked, jnp.zeros_like(picked))
-    gathered_slots = lax.all_gather(slot_rows, "frames", axis=1, tiled=True)
+    ways, here = (lax.axis_size("frames"), lax.axis_index("frames"))
+    grown, reach = (slot_rows, 1)
+    while reach < ways:
+        theirs = lax.ppermute(grown, "frames", [(d, d ^ reach) for d in range(ways)])
+        mine_first = jnp.concatenate([grown, theirs], axis=1)
+        theirs_first = jnp.concatenate([theirs, grown], axis=1)
+        grown = jnp.where(here & reach == 0, mine_first, theirs_first)
+        reach = 2 * reach
+    gathered_slots = grown
     sequence_order = sequence_slots(all_counts, devices * TOKL, KMAX)
     local_cols = jnp.dot(
         gathered_slots.reshape(-1, model_width), w_proj, preferred_element_type=jnp.float32

time: 197 us -> 193 us (0.980)
  blocking collectives: 89.1 us -> 68.1 us
  waiting for transfers between devices: 33.6 us -> 45.1 us
  starting transfers between devices: 4.46 us -> 9.94 us
    all_gather x1 -> x0, blocking collectives: 20.6 us -> none  [local(): gathered_slots = lax.all_gather(slot_rows, 'frames', axis=1, tiled=True)]
    ppermute x0 -> x4, waiting for transfers between devices: none -> 11.4 us  [local(): lax.ppermute(grown, 'frames', [(d, d ^ reach) for d in range(ways)])]
    ppermute x0 -> x4, starting transfers between devices: none -> 5.48 us  [local(): lax.ppermute(grown, 'frames', [(d, d ^ reach) for d in range(ways)])]
  transfers between devices with their start and end apart: 2 -> 6, of which waited for: 2 -> 6; matrix products, arithmetic and copies ran while one was open for 1% -> 1% of each run, Pallas kernels for 0% -> 0%
where the time goes in v1:
time: 193 us; the launch traced here: 192 us
  blocking collectives  68.1 us (35%)
  waiting for transfers between devices  45.1 us (23%)
  matrix products  32.3 us (17%)
  local copies, waits for them, and re-layouts  14.8 us (8%)
  between operations  13.6 us (7%)
  starting transfers between devices  9.94 us (5%)
  other arithmetic  8.12 us (4%)
    psum x1, blocking collectives, local(): squares = lax.psum(jnp.sum(local_cols * local_cols, axis=2), 'frames')  29.5 us
    all_to_all x1, blocking collectives, local(): lax.all_to_all(normed, 'frames', split_axis=2, concat_axis=1, tiled=True)  21.5 us
    all_gather x1, waiting for transfers between devices, local(): column_piece = lax.all_gather(normed_cols, 'frames', axis=2, tiled=True)  20.8 us
    all_gather x1, blocking collectives, local(): all_counts = lax.all_gather(kept_counts, 'frames', axis=1, tiled=True)  17.2 us
    all_to_all x1, waiting for transfers between devices, local(): lax.all_to_all(attended, 'frames', split_axis=1, concat_axis=2, tiled=True)  13 us
    ppermute x4, waiting for transfers between devices, local(): lax.ppermute(grown, 'frames', [(d, d ^ reach) for d in range(ways)])  11.4 us
    dot_general x1, matrix products, local(): jnp.dot(flat_piece, w_gate, preferred_element_type=jnp.float32)  8.87 us
    dot_general x1, matrix products, local(): jnp.dot(flat_piece, w_up, preferred_element_type=jnp.float32)  8.34 us
  transfers between devices with their start and end apart: 6, of which 6 were waited for; matrix products, arithmetic and copies ran while one was open for 1% of the time, Pallas kernels for 0%

profile of v1, /device:TPU:0, one launch (start us, length us, event | category | flops | bytes accessed | tf_op | source)
XLA Modules:
  0.0 192.0 jit_solution(10095998272529131313)
XLA Ops:
  6.5 0.0 copy-start
  6.5 1.7 convert_reduce_fusion
  8.3 1.9 %multiply_reduce_fusion.1 = f32[2,128]{0,1:T(8,128)S(1)} fusion(f32[2,128]{0,1:T(8,128)S(1)} %broadcast_multiply_fusion, bf16[2,1,128,1024]{3,2,1,0:T(8,128)(2,1)} %param.9), kind=kLoop, calls=%fused_computation.27 | loop fusion | flops 1048320 | bytes 526336 | tf_op jit(solution)/shard_map/reduce_sum | solution.py:18
  10.2 1.7 multiply_convert_fusion
  12.0 21.5 %all_to_all.8 = bf16[2,1,128,1024]{3,0,1,2:T(2,128)(2,1)S(1)} all-to-all(bf16[2,1,128,1024]{3,0,1,2:T(2,128)(2,1)S(1)} %multiply_convert_fusion), channel_id=1, replica_groups=mesh['groups'=2,'frames'=16] {'frames'}, dimensions={2} | all-to-all | bytes 1048576 | tf_op jit(solution)/shard_map/all_to_all | solution.py:63
  33.5 0.1 copy.52
  33.6 4.6 %convolution_convert_fusion = bf16[256,3072]{1,0:T(8,128)(2,1)S(1)} fusion(bf16[256,1024]{1,0:T(8,128)(2,1)S(1)} %bitcast.65, bf16[1024,3072]{1,0:T(8,128)(2,1)} %param.10), kind=kOutput, calls=%fused_computation.7 | convolution fusion | flops 1611399168 | bytes 8388608 | tf_op jit(solution)/shard_map/dot_general | solution.py:64
  38.2 0.9 fusion.48
  39.1 2.5 %reshape.178 = bf16[2,16,8,16,64]{4,3,2,1,0:T(8,128)(2,1)} reshape(bf16[2,16,8,1024]{3,2,1,0:T(8,128)(2,1)} %get-tuple-element.7) | data formatting | bytes 1048576 | tf_op jit(solution)/shard_map/reshape | solution.py:61
  41.6 1.6 reshape.179
  43.2 1.6 reshape.177
  44.9 0.0 copy-start.3
  44.9 4.9 %fusion.49 = (f32[2,8,16,16]{3,2,1,0:T(8,128)S(1)}, f32[2,8,16,16,16]{3,4,2,1,0:T(8,128)}) fusion(bf16[2,16,8,16,64]{4,3,2,1,0:T(8,128)(2,1)} %reshape.179, bf16[2,16,8,16,64]{4,3,2,1,0:T(8,128)(2,1)} %reshape.178), kind=kOutput, calls=%fused_computation.71 | convolution fusion | flops 8585231 | bytes 1327104 | tf_op jit(solution)/shard_map/sub | solution.py:40
  49.8 0.0 copy-done.3
  49.8 2.5 %fusion.6 = bf16[2,16,8,16,64]{4,1,3,2,0:T(8,128)(2,1)S(1)} fusion(f32[2,8,16,16,16]{3,4,2,1,0:T(8,128)} %get-tuple-element.9, bf16[2,16,8,16,64]{4,3,2,1,0:T(8,128)(2,1)S(1)} %copy-done.3, f32[2,8,16,16]{3,2,1,0:T(8,128)S(1)} %get-tuple-element.8), kind=kOutput, calls=%fused_computation.13 | convolution fusion | flops 8781824 | bytes 1327104 | tf_op jit(solution)/shard_map/vphfg,vgphe->vfphe/dot_general | solution.py:42
  52.2 0.0 copy-start.2
  52.3 1.3 copy.61
  53.5 2.6 %reshape.202 = bf16[2,16,8,1024]{3,2,0,1:T(8,128)(2,1)} reshape(bf16[2,16,8,16,64]{4,3,2,0,1:T(8,128)(2,1)} %copy.61) | data formatting | bytes 1048576 | tf_op jit(solution)/shard_map/reshape | solution.py:72
  56.1 4.2 %all-to-all-start.1 = ((bf16[2,16,8,1024]{3,2,0,1:T(8,128)(2,1)}), bf16[2,16,8,1024]{3,2,0,1:T(8,128)(2,1)}, u32[]{:S(2)}, u32[]{:S(2)}) async-start(bf16[2,16,8,1024]{3,2,0,1:T(8,128)(2,1)} %reshape.202), calls=%async_computation.1 | async-start | bytes 1048576 | tf_op jit(solution)/shard_map/all_to_all | solution.py:73
  60.4 0.0 copy-start.5
  60.4 0.0 copy-start.6
  60.4 0.2 all-gather.3.cloned.1.call-start
  60.6 0.0 copy-done.2
  60.6 0.5 copy_convert_fusion
  61.2 0.3 copy.51
  61.5 0.0 copy-done.5
  61.5 0.1 reshape.183
  61.6 0.0 copy-done.6
  61.6 0.1 iota_compare_fusion.2
  61.7 13.0 %all-to-all-done.1 = bf16[2,16,8,1024]{3,2,0,1:T(8,128)(2,1)} async-done(((bf16[2,16,8,1024]{3,2,0,1:T(8,128)(2,1)}), bf16[2,16,8,1024]{3,2,0,1:T(8,128)(2,1)}, u32[]{:S(2)}, u32[]{:S(2)}) %all-to-all-start.1) | async-done | bytes 524320 | tf_op jit(solution)/shard_map/all_to_all | solution.py:73
  74.7 1.1 copy.59
  75.7 0.0 copy-done
  75.8 0.0 copy-start.4
  75.8 1.5 fusion.7
  77.3 1.3 gather_fusion
  78.6 0.1 select_select_fusion
  78.7 0.2 collective-permute-start
  78.9 1.0 collective-permute-done
  80.0 1.1 collective-permute-start.1
  81.1 2.8 %collective-permute-done.1 = bf16[2,8,1024]{2,1,0:T(8,128)(2,1)S(1)} collective-permute-done((bf16[2,8,1024]{2,1,0:T(8,128)(2,1)S(1)}, bf16[2,8,1024]{2,1,0:T(8,128)(2,1)S(1)}, u32[]{:S(2)}, u32[]{:S(2)}) %collective-permute-start.1) | collective-permute-done | bytes 32800 | tf_op jit(solution)/shard_map/ppermute | solution.py:87
  84.0 1.6 collective-permute-start.2
  85.6 2.7 %collective-permute-done.2 = bf16[2,16,1024]{2,1,0:T(8,128)(2,1)S(1)} collective-permute-done((bf16[2,16,1024]{2,1,0:T(8,128)(2,1)S(1)}, bf16[2,16,1024]{2,1,0:T(8,128)(2,1)S(1)}, u32[]{:S(2)}, u32[]{:S(2)}) %collective-permute-start.2) | collective-permute-done | bytes 65568 | tf_op jit(solution)/shard_map/ppermute | solution.py:87
  88.3 2.5 %collective-permute-start.3 = (bf16[2,32,1024]{2,1,0:T(8,128)(2,1)S(1)}, bf16[2,32,1024]{2,1,0:T(8,128)(2,1)S(1)}, u32[]{:S(2)}, u32[]{:S(2)}) collective-permute-start(bf16[2,32,1024]{2,1,0:T(8,128)(2,1)S(1)} %maximum_select_fusion.2), channel_id=1, source_target_pairs={{0,8},{1,9},{2,10},{3,11},{4,12},{5,13},{6,14},{7,15},{8,0},{9,1},... | collective-permute-start | bytes 393224 | tf_op jit(solution)/shard_map/ppermute | solution.py:87
  90.8 0.0 copy-done.4
  90.8 4.8 %collective-permute-done.3 = bf16[2,32,1024]{2,1,0:T(8,128)(2,1)S(1)} collective-permute-done((bf16[2,32,1024]{2,1,0:T(8,128)(2,1)S(1)}, bf16[2,32,1024]{2,1,0:T(8,128)(2,1)S(1)}, u32[]{:S(2)}, u32[]{:S(2)}) %collective-permute-start.3) | collective-permute-done | bytes 131104 | tf_op jit(solution)/shard_map/ppermute | solution.py:87
  95.7 1.6 multiply_reduce_fusion.2
  97.3 29.5 %psum.7 = f32[2,64]{1,0:T(2,128)S(1)} all-reduce(f32[2,64]{1,0:T(2,128)S(1)} %get-tuple-element.10), channel_id=1, replica_groups=mesh['groups'=2,'frames'=16] {'frames'}, use_global_device_ids=true, to_apply=%region_8.9 | all-reduce | flops 128 | bytes 1024 | tf_op jit(solution)/shard_map/psum | solution.py:98
  126.8 0.8 multiply_convert_fusion.1
  127.5 0.0 all-gather.3.cloned.1.call-update
  127.6 17.2 %all-gather = s32[16,1,2]{2,1,0:T(1,128)S(1)} all-gather(s32[1,1,2]{2,1,0:T(1,128)S(1)} %bitcast.70), channel_id=1, replica_groups=mesh['groups'=2,'frames'=16] {'frames'}, dimensions={0}, use_global_device_ids=true | all-gather | bytes 136 | tf_op jit(solution)/shard_map/all_gather | solution.py:57
  144.7 0.1 copy.49
  144.8 0.2 reduce_window_sum.11
  145.0 0.1 convert_reduce_fusion.1
  145.1 0.1 select_reduce_fusion
  145.2 0.1 reshape.189
  145.3 20.8 %all-gather.3.cloned.1.call-done = bf16[2,64,8192]{2,1,0:T(8,128)(2,1)} async-done(((bf16[2,64,512]{2,1,0:T(8,128)(2,1)}), bf16[2,64,8192]{2,1,0:T(8,128)(2,1)}) %all-gather.3.cloned.1.call-update) | async-done | bytes 2097168 | tf_op jit(solution)/shard_map/all_gather | solution.py:107
  166.0 0.0 copy-start.1
  166.0 8.9 %fusion.3 = f32[2,64,1024]{2,1,0:T(8,128)S(1)} fusion(bf16[2,64,8192]{2,1,0:T(8,128)(2,1)} %all-gather.3.cloned.1.call-done, bf16[8192,1024]{1,0:T(8,128)(2,1)} %param.16), kind=kOutput, calls=%fused_computation.5 | convolution fusion | flops 2147483648 | bytes 19398656 | tf_op jit(solution)/shard_map/dot_general | solution.py:110
  174.9 0.0 copy-done.1
  174.9 8.3 %fusion.11 = bf16[2,64,1024]{2,1,0:T(8,128)(2,1)S(1)} fusion(bf16[2,64,8192]{2,1,0:T(8,128)(2,1)S(1)} %copy-done.1, bf16[8192,1024]{1,0:T(8,128)(2,1)} %param.17, f32[2,64,1024]{2,1,0:T(8,128)S(1)} %fusion.3), kind=kOutput, calls=%fused_computation.17 | convolution fusion | flops 2148270080 | bytes 19660800 | tf_op jit(solution)/shard_map/dot_general | solution.py:113
  183.3 1.1 gather_fusion.1
  184.4 0.7 broadcast_select_fusion
  (14 shorter events, 0.2 us)
Async XLA Ops:
  6.5 69.2 %copy-start = (bf16[1024,1024]{1,0:T(8,128)(2,1)S(1)}, bf16[1024,1024]{1,0:T(8,128)(2,1)}, u32[]{:S(2)}) copy-start(bf16[1024,1024]{1,0:T(8,128)(2,1)} %param.11) | copy-start | bytes 6291460
  44.9 4.9 %copy-start.3 = (bf16[2,16,8,16,64]{4,3,2,1,0:T(8,128)(2,1)S(1)}, bf16[2,16,8,16,64]{4,3,2,1,0:T(8,128)(2,1)}, u32[]{:S(2)}) copy-start(bf16[2,16,8,16,64]{4,3,2,1,0:T(8,128)(2,1)} %reshape.177) | copy-start | bytes 1572868
  52.2 8.4 %copy-start.2 = (bf16[2,1,128,1024]{3,2,1,0:T(8,128)(2,1)S(1)}, bf16[2,1,128,1024]{3,2,1,0:T(8,128)(2,1)}, u32[]{:S(2)}) copy-start(bf16[2,1,128,1024]{3,2,1,0:T(8,128)(2,1)} %param.9) | copy-start | bytes 1572868
  56.1 18.5 %all-to-all-start.1 = ((bf16[2,16,8,1024]{3,2,0,1:T(8,128)(2,1)}), bf16[2,16,8,1024]{3,2,0,1:T(8,128)(2,1)}, u32[]{:S(2)}, u32[]{:S(2)}) async-start(bf16[2,16,8,1024]{3,2,0,1:T(8,128)(2,1)} %reshape.202), calls=%async_computation.1 | async-start | bytes 1048576 | tf_op jit(solution)/shard_map/all_to_all | solution.py:73
  60.4 1.2 copy-start.5
  60.4 1.3 copy-start.6
  60.4 105.6 %all-gather.3.cloned.1.call-start = ((), (), s32[]{:S(2)}) async-start(), calls=%async_computation.2 | async-start | bytes 2228224 | tf_op jit(solution)/shard_map/all_gather | solution.py:107
  75.8 15.1 %copy-start.4 = (bf16[512]{0:T(512)(128)(2,1)S(1)}, bf16[512]{0:T(512)(128)(2,1)}, u32[]{:S(2)}) copy-start(bf16[512]{0:T(512)(128)(2,1)} %param.15) | copy-start | bytes 3076
  78.7 1.2 collective-permute-start
  80.0 4.0 %collective-permute-start.1 = (bf16[2,8,1024]{2,1,0:T(8,128)(2,1)S(1)}, bf16[2,8,1024]{2,1,0:T(8,128)(2,1)S(1)}, u32[]{:S(2)}, u32[]{:S(2)}) collective-permute-start(bf16[2,8,1024]{2,1,0:T(8,128)(2,1)S(1)} %maximum_select_fusion.4), channel_id=1, source_target_pairs={{0,2},{1,3},{2,0},{3,1},{4,6},{5,7},{6,4},{7,5},{8,10},{9,11},{10,... | collective-permute-start | bytes 98312 | tf_op jit(solution)/shard_map/ppermute | solution.py:87
  84.0 4.3 %collective-permute-start.2 = (bf16[2,16,1024]{2,1,0:T(8,128)(2,1)S(1)}, bf16[2,16,1024]{2,1,0:T(8,128)(2,1)S(1)}, u32[]{:S(2)}, u32[]{:S(2)}) collective-permute-start(bf16[2,16,1024]{2,1,0:T(8,128)(2,1)S(1)} %maximum_select_fusion.3), channel_id=1, source_target_pairs={{0,4},{1,5},{2,6},{3,7},{4,0},{5,1},{6,2},{7,3},{8,12},{9,13},{10,... | collective-permute-start | bytes 196616 | tf_op jit(solution)/shard_map/ppermute | solution.py:87
  88.3 7.3 %collective-permute-start.3 = (bf16[2,32,1024]{2,1,0:T(8,128)(2,1)S(1)}, bf16[2,32,1024]{2,1,0:T(8,128)(2,1)S(1)}, u32[]{:S(2)}, u32[]{:S(2)}) collective-permute-start(bf16[2,32,1024]{2,1,0:T(8,128)(2,1)S(1)} %maximum_select_fusion.2), channel_id=1, source_target_pairs={{0,8},{1,9},{2,10},{3,11},{4,12},{5,13},{6,14},{7,15},{8,0},{9,1},... | collective-permute-start | bytes 393224 | tf_op jit(solution)/shard_map/ppermute | solution.py:87
  166.0 8.9 %copy-start.1 = (bf16[2,64,8192]{2,1,0:T(8,128)(2,1)S(1)}, bf16[2,64,8192]{2,1,0:T(8,128)(2,1)}, u32[]{:S(2)}) copy-start(bf16[2,64,8192]{2,1,0:T(8,128)(2,1)} %all-gather.3.cloned.1.call-done) | copy-start | bytes 6291460
Sparse Core Ops, SparseCore 0:
  127.7 38.3 all-gather.2
